TPU v7x, 512 devices: a whole 4x8x8 slice. The times are simulated.
512 devices in a mesh: blk: 8 (over z_lo, core), owner: 64 (over z_hi, x, y).
Axes of the slice: x: 4, y: 8, z: 8 (z_hi: 2, z_lo: 4; z = z_hi * 4 + z_lo), core: 2. Of those that a mesh axis runs over, the one named last changes fastest.
Arguments:
- tokens: bfloat16 [2048, 32, 1024], P(('owner', 'blk')), may hold values from -6 to 6
- w_qkv: bfloat16 [1024, 3, 1024], P(None, None, 'blk'), may hold values from -0.1875 to 0.1875
- w_out: bfloat16 [1024, 1024], P('blk'), may hold values from -0.5625 to 0.5625
- b_out: bfloat16 [1024], replicated, may hold values from -3 to 3
- gain1: bfloat16 [1024], replicated, may hold values from 0.5 to 1.5
- shift1: bfloat16 [1024], replicated, may hold values from -2 to 2
- w_up: bfloat16 [1024, 4096], P(None, 'blk'), may hold values from -0.1875 to 0.1875
- b_up: bfloat16 [4096], P('blk'), may hold values from -3 to 3
- w_down: bfloat16 [4096, 1024], P('blk'), may hold values from -0.09375 to 0.09375
- b_down: bfloat16 [1024], replicated, may hold values from -3 to 3
- gain2: bfloat16 [1024], replicated, may hold values from 0.5 to 1.5
- shift2: bfloat16 [1024], replicated, may hold values from -2 to 2
- root_cache: bfloat16 [2, 4, 1024, 1024], P(None, None, 'owner', 'blk'), may hold values from -90 to 90
- node_cache: bfloat16 [2, 128, 384, 1024], P(None, 'owner', None, 'blk'), may hold values from -90 to 90
- root_len: int32 [4], replicated, may hold values from 128 to 1024
- node_len: int32 [128], replicated, may hold values from 48 to 384
- node_parent: int32 [128], replicated, may hold values from 0 to 31, as said below
- node_place: int32 [128], replicated, may hold values from 0 to 127, as said below
- req_leaf: int32 [2048], P('owner'), may hold values from 32 to 127, as said below
Outputs:
- result: bfloat16 [2048, 32, 1024], P(('owner', 'blk'))
- new_caches: bfloat16 [2, 2048, 32, 1024], P(None, 'owner', None, 'blk')
Inputs may be any that keep to these rules, and one draw needn't show every extreme that they name: `node_parent`: entries below 32 are branch nodes and name their tenant; each other entry is a leaf and names its branch node; every branch node has exactly three leaves. `node_place`: a permutation of the pool slots; slot s lies on owner s // 2. `req_leaf`: always a leaf; the requests of one owner index lie below different branch nodes.
All inputs are finite; a program needn't handle non-finite values.
Results may differ from a plain program's by a relative error of at most 0.02.
Values may be sent and summed in bfloat16 or wider, within the bound.
No kernel may reach another device: no remote copies, remote signals or barrier semaphores. Data moves between devices by JAX's collectives and lax.ppermute only.
A program may use at most 128 MiB of HBM per device.

v0:
```python
import math
import jax
import jax.numpy as jnp
from jax import lax
from jax.sharding import PartitionSpec as P

HD = 64
norm_eps = 1e-05
masked_score = -1e30


def layer_norm(values, gain, shift):
    center = values - jnp.mean(values, axis=-1, keepdims=True)
    spread = jnp.mean(center * center, axis=-1, keepdims=True)
    return center * lax.rsqrt(spread + norm_eps) * gain.astype(jnp.float32) + shift.astype(
        jnp.float32
    )


def attend_own(queries, key_rows, value_rows, score_scale):
    scores = (
        jnp.einsum("rshe,rnhe->rshn", queries, key_rows, preferred_element_type=jnp.float32)
        * score_scale
    )
    peak = jnp.max(scores, axis=-1)
    weights = jnp.exp(scores - peak[..., None])
    weight_sum = jnp.sum(weights, axis=-1)
    mixed = jnp.einsum(
        "rshn,rnhe->rshe",
        weights.astype(jnp.bfloat16),
        value_rows,
        preferred_element_type=jnp.float32,
    )
    return (mixed / weight_sum[..., None], peak + jnp.log(weight_sum))


def on_device(
    tokens,
    w_qkv,
    w_out,
    b_out,
    gain1,
    shift1,
    w_up,
    b_up,
    w_down,
    b_down,
    gain2,
    shift2,
    root_cache,
    node_cache,
    root_len,
    node_len,
    node_parent,
    node_place,
    req_leaf,
):
    req_dev, suffix, model_width = tokens.shape
    head_cols = w_qkv.shape[2]
    local_heads = head_cols // HD
    own_rows = req_dev * suffix
    owners = lax.axis_size("owner")
    group_size = req_leaf.shape[0]
    score_scale = 1.0 / math.sqrt(HD)
    flat_qkv = w_qkv.reshape(model_width, 3 * head_cols)
    shard_rows = lax.all_gather(tokens, "blk", axis=0, tiled=True)
    row_count = shard_rows.shape[0]
    mixed = jnp.dot(
        shard_rows.reshape(row_count * suffix, model_width),
        flat_qkv,
        preferred_element_type=jnp.float32,
    )
    projected = mixed.astype(jnp.bfloat16).reshape(row_count, suffix, 3 * head_cols)
    queries = projected[:, :, :head_cols].reshape(group_size, suffix, local_heads, HD)
    keys_new = projected[:, :, head_cols : 2 * head_cols]
    values_new = projected[:, :, 2 * head_cols :]
    new_caches = jnp.stack([keys_new, values_new])
    branch = node_parent[req_leaf]
    tenant = node_parent[branch]
    root_limit = root_len[tenant]
    roots_all = lax.all_gather(root_cache, "owner", axis=2, tiled=True)
    root_rows = roots_all.shape[2]
    block_len = math.gcd(root_rows, 256)

    def root_block(block_index, state):
        peak, weight_sum, weighted = state
        offset = block_index * block_len
        key_rows = lax.dynamic_slice_in_dim(roots_all[0], offset, block_len, 1)
        value_rows = lax.dynamic_slice_in_dim(roots_all[1], offset, block_len, 1)
        key_block = jnp.take(key_rows, tenant, axis=0).reshape(
            group_size, block_len, local_heads, HD
        )
        value_block = jnp.take(value_rows, tenant, axis=0).reshape(
            group_size, block_len, local_heads, HD
        )
        positions = offset + jnp.arange(block_len, dtype=jnp.int32)
        in_range = (positions[None, :] < root_limit[:, None])[:, None, None, :]
        scores = (
            jnp.einsum("rshe,rnhe->rshn", queries, key_block, preferred_element_type=jnp.float32)
            * score_scale
        )
        scores = jnp.where(in_range, scores, masked_score)
        new_peak = jnp.maximum(peak, jnp.max(scores, axis=-1))
        weights = jnp.where(in_range, jnp.exp(scores - new_peak[..., None]), 0.0)
        factor = jnp.exp(peak - new_peak)
        weight_sum = weight_sum * factor + jnp.sum(weights, axis=-1)
        weighted = weighted * factor[..., None] + jnp.einsum(
            "rshn,rnhe->rshe",
            weights.astype(jnp.bfloat16),
            value_block,
            preferred_element_type=jnp.float32,
        )
        return (new_peak, weight_sum, weighted)

    start_state = (
        jnp.full((group_size, suffix, local_heads), masked_score, jnp.float32),
        jnp.zeros((group_size, suffix, local_heads), jnp.float32),
        jnp.zeros((group_size, suffix, local_heads, HD), jnp.float32),
    )
    root_peak, root_sum, root_weighted = lax.fori_loop(
        0, root_rows // block_len, root_block, start_state
    )
    root_out = root_weighted / root_sum[..., None]
    root_mass = root_peak + jnp.log(root_sum)
    slot_total = node_place.shape[0]
    slot_count = slot_total // owners
    node_max = node_cache.shape[2]
    slot_ids = jnp.arange(slot_total, dtype=jnp.int32)
    at_branch = slot_ids[:, None] == node_place[branch][None, :]
    at_leaf = slot_ids[:, None] == node_place[req_leaf][None, :]
    route = (at_branch | at_leaf).astype(jnp.bfloat16)
    outgoing = jnp.dot(
        route, queries.reshape(group_size, suffix * head_cols), preferred_element_type=jnp.float32
    )
    outgoing = outgoing.astype(jnp.bfloat16).reshape(owners, slot_count, suffix, head_cols)
    slot_len = jnp.sum(
        jnp.where(slot_ids[:, None] == node_place[None, :], node_len[None, :], 0), axis=1
    )
    my_owner = lax.axis_index("owner")
    local_len = lax.dynamic_slice_in_dim(slot_len, my_owner * slot_count, slot_count)
    cache_keys = node_cache[0].reshape(slot_count, node_max, local_heads, HD)
    cache_values = node_cache[1].reshape(slot_count, node_max, local_heads, HD)
    local_range = jnp.arange(node_max, dtype=jnp.int32)[None, :] < local_len[:, None]
    incoming = lax.all_to_all(outgoing, "owner", split_axis=0, concat_axis=0, tiled=True)
    sources, _, row_count, _ = incoming.shape
    block_width = 8
    blocks = incoming.reshape(
        sources // block_width, block_width, slot_count, row_count, local_heads, HD
    )

    def source_block(block_queries):
        scores = (
            jnp.einsum(
                "bkthe,knhe->bkthn", block_queries, cache_keys, preferred_element_type=jnp.float32
            )
            * score_scale
        )
        keep_rows = local_range[None, :, None, None, :]
        scores = jnp.where(keep_rows, scores, masked_score)
        peak = jnp.max(scores, axis=-1)
        weights = jnp.where(keep_rows, jnp.exp(scores - peak[..., None]), 0.0)
        weight_sum = jnp.sum(weights, axis=-1)
        mixed = jnp.einsum(
            "bkthn,knhe->bkthe",
            weights.astype(jnp.bfloat16),
            cache_values,
            preferred_element_type=jnp.float32,
        )
        mixed = mixed / weight_sum[..., None]
        return (
            mixed.reshape(block_width, slot_count, row_count, head_cols),
            peak + jnp.log(weight_sum),
        )

    mixed, log_mass = lax.map(source_block, blocks)
    mixed = mixed.reshape(sources, slot_count, row_count, head_cols)
    log_mass = log_mass.reshape(sources, slot_count, row_count, local_heads)
    back_out = lax.all_to_all(mixed, "owner", split_axis=0, concat_axis=0, tiled=True)
    back_mass = lax.all_to_all(log_mass, "owner", split_axis=0, concat_axis=0, tiled=True)
    back_flat = back_out.reshape(slot_total, suffix * head_cols)
    mass_flat = back_mass.reshape(slot_total, suffix * local_heads)

    def collect(selected):
        weights_sel = selected.astype(jnp.float32)
        gathered = jnp.einsum("gr,gf->rf", weights_sel, back_flat, precision=lax.Precision.HIGHEST)
        masses = jnp.einsum("gr,gf->rf", weights_sel, mass_flat, precision=lax.Precision.HIGHEST)
        return (
            gathered.reshape(group_size, suffix, local_heads, HD),
            masses.reshape(group_size, suffix, local_heads),
        )

    branch_out, branch_mass = collect(at_branch)
    leaf_out, leaf_mass = collect(at_leaf)
    own_out, own_mass = attend_own(
        queries,
        keys_new.reshape(group_size, suffix, local_heads, HD),
        values_new.reshape(group_size, suffix, local_heads, HD),
        score_scale,
    )
    set_outs = [root_out, branch_out, leaf_out, own_out]
    set_masses = [root_mass, branch_mass, leaf_mass, own_mass]
    highest = jnp.maximum(jnp.maximum(root_mass, branch_mass), jnp.maximum(leaf_mass, own_mass))
    mass_sum = (
        jnp.exp(root_mass - highest)
        + jnp.exp(branch_mass - highest)
        + jnp.exp(leaf_mass - highest)
        + jnp.exp(own_mass - highest)
    )
    total = highest + jnp.log(mass_sum)
    attn = set_outs[0] * jnp.exp(set_masses[0] - total)[..., None]
    for set_index in range(1, 4):
        attn = attn + set_outs[set_index] * jnp.exp(set_masses[set_index] - total)[..., None]
    attn = attn.astype(jnp.bfloat16).reshape(group_size, suffix, head_cols)
    attn_flat = attn.reshape(group_size * suffix, head_cols)
    head_sum = lax.psum_scatter(
        jnp.dot(attn_flat, w_out, preferred_element_type=jnp.float32).astype(jnp.bfloat16),
        "blk",
        scatter_dimension=0,
        tiled=True,
    ).astype(jnp.float32)
    first_norm = layer_norm(
        tokens.reshape(own_rows, model_width).astype(jnp.float32)
        + head_sum
        + b_out.astype(jnp.float32),
        gain1,
        shift1,
    ).astype(jnp.bfloat16)
    inner_act = jnp.dot(
        lax.all_gather(first_norm, "blk", axis=0, tiled=True),
        w_up,
        preferred_element_type=jnp.float32,
    ) + b_up.astype(jnp.float32)
    hidden = jax.nn.gelu(inner_act, approximate=False).astype(jnp.bfloat16)
    down_sum = lax.psum_scatter(
        jnp.dot(hidden, w_down, preferred_element_type=jnp.float32).astype(jnp.bfloat16),
        "blk",
        scatter_dimension=0,
        tiled=True,
    ).astype(jnp.float32)
    result = layer_norm(
        first_norm.astype(jnp.float32) + down_sum + b_down.astype(jnp.float32), gain2, shift2
    ).astype(jnp.bfloat16)
    return (result.reshape(req_dev, suffix, model_width), new_caches)


def solution(mesh):
    in_specs = (
        P(("owner", "blk"), None, None),
        P(None, None, "blk"),
        P("blk", None),
        P(),
        P(),
        P(),
        P(None, "blk"),
        P("blk"),
        P("blk", None),
        P(),
        P(),
        P(),
        P(None, None, "owner", "blk"),
        P(None, "owner", None, "blk"),
        P(),
        P(),
        P(),
        P(),
        P("owner"),
    )
    out_specs = (P(("owner", "blk"), None, None), P(None, "owner", None, "blk"))
    return jax.shard_map(
        on_device, mesh=mesh, in_specs=in_specs, out_specs=out_specs, check_vma=False
    )
```

profile of v0, /device:TPU:2, one launch (start us, length us, event | category | flops | bytes accessed | tf_op | source)
XLA Modules:
  0.0 547.2 jit_solution(3773147124506278843)
XLA Ops:
  13.0 44.8 %all-gather.6.cloned.1.call-done = bf16[32,32,1024]{2,1,0:T(8,128)(2,1)} async-done(((bf16[4,32,1024]{2,1,0:T(8,128)(2,1)}), bf16[32,32,1024]{2,1,0:T(8,128)(2,1)}) %all-gather.6.cloned.1.call-update) | async-done | bytes 2097168 | tf_op jit(solution)/shard_map/all_gather | solution.py:66
  63.4 14.2 %all-to-all-start = ((bf16[64,2,32,128]{3,2,1,0:T(8,128)(2,1)}), bf16[64,2,32,128]{3,2,1,0:T(8,128)(2,1)}, u32[]{:S(2)}, u32[]{:S(2)}) async-start(bf16[64,2,32,128]{3,2,1,0:T(8,128)(2,1)} %bitcast.57), calls=%async_computation | async-start | bytes 2097152 | tf_op jit(solution)/shard_map/all_to_all | solution.py:144
  88.7 18.2 %all-to-all-done = bf16[64,2,32,128]{3,2,1,0:T(8,128)(2,1)} async-done(((bf16[64,2,32,128]{3,2,1,0:T(8,128)(2,1)}), bf16[64,2,32,128]{3,2,1,0:T(8,128)(2,1)}, u32[]{:S(2)}, u32[]{:S(2)}) %all-to-all-start) | async-done | bytes 1048608 | tf_op jit(solution)/shard_map/all_to_all | solution.py:144
  107.0 5.0 reshape.205
  112.0 39.3 %while.31 = (s32[]{:T(128)}, f32[8,8,2,32,128]{4,3,2,1,0:T(8,128)}, f32[8,8,2,32,2]{3,1,0,4,2:T(8,128)}, bf16[8,8,2,32,2,64]{5,4,3,2,1,0:T(2,128)(2,1)}, bf16[2,...) while((s32[]{:T(128)}, f32[8,8,2,32,128]{4,3,2,1,0:T(8,128)}, ...), condition=%wide.region_8.10_spmd.clone, body=%wide.region_5.9_spmd.clone.sunk | while | flops 104267520 | bytes 7389281 | solution.py:175
  153.1 7.8 %all-to-all-start.1 = ((f32[64,1,128]{2,1,0:T(1,128)}), f32[64,1,128]{2,1,0:T(1,128)S(1)}, u32[]{:S(2)}, u32[]{:S(2)}) async-start(f32[64,1,128]{2,1,0:T(1,128)} %reshape.304), calls=%async_computation.1 | async-start | bytes 65536 | tf_op jit(solution)/shard_map/all_to_all | solution.py:179
  163.9 10.5 %all-to-all-done.1 = f32[64,1,128]{2,1,0:T(1,128)S(1)} async-done(((f32[64,1,128]{2,1,0:T(1,128)}), f32[64,1,128]{2,1,0:T(1,128)S(1)}, u32[]{:S(2)}, u32[]{:S(2)}) %all-to-all-start.1) | async-done | bytes 32800 | tf_op jit(solution)/shard_map/all_to_all | solution.py:179
  175.0 6.4 %all-to-all-start.2 = ((f32[64,2,32,128]{3,2,1,0:T(8,128)}), f32[64,2,32,128]{3,2,1,0:T(8,128)}, u32[]{:S(2)}, u32[]{:S(2)}) async-start(f32[64,2,32,128]{3,2,1,0:T(8,128)} %bitcast.197), calls=%async_computation.2 | async-start | bytes 4194304 | tf_op jit(solution)/shard_map/all_to_all | solution.py:178
  181.6 88.1 %all-gather.4.cloned.1.call-done = bf16[2,4,1024,128]{3,2,1,0:T(8,128)(2,1)} async-done(((bf16[2,4,16,128]{3,2,1,0:T(8,128)(2,1)}), bf16[2,4,1024,128]{3,2,1,0:T(8,128)(2,1)}) %all-gather.4.cloned.1.call-update) | async-done | bytes 2097168 | tf_op jit(solution)/shard_map/all_gather | solution.py:81
  269.7 106.4 %while.32 = (s32[]{:T(128)}, f32[32,32,2]{1,2,0:T(2,128)S(1)}, f32[32,32,2]{1,2,0:T(2,128)S(1)}, f32[32,32,2,64]{3,1,2,0:T(8,128)}, s32[32]{0:T(128)S(1)}, /*ind...) while((s32[]{:T(128)}, f32[32,32,2]{1,2,0:T(2,128)S(1)}, ...), condition=%wide.region_3.5_spmd.clone, body=%wide.region_0.4_spmd.clone.sunk | while | flops 143543840 | bytes 50766020 | solution.py:120
  276.5 4.1 broadcast_select_fusion.4
  280.6 4.1 copy.240
  288.1 4.1 copy.241
  292.2 4.0 fusion.189
  303.0 4.1 broadcast_select_fusion.4
  307.1 4.1 copy.240
  314.6 4.1 copy.241
  318.8 4.0 fusion.189
  329.6 4.1 broadcast_select_fusion.4
  333.7 4.1 copy.240
  341.3 4.1 copy.241
  345.4 4.0 fusion.189
  356.3 4.1 broadcast_select_fusion.4
  360.4 4.1 copy.240
  367.9 4.1 copy.241
  372.0 4.0 fusion.189
  387.4 5.2 fusion.43
  392.7 4.0 fusion.46
  399.7 38.1 %reduce-scatter.3.cloned.1.call-done = bf16[128,1024]{1,0:T(8,128)(2,1)} async-done(((bf16[1024,1024]{1,0:T(8,128)(2,1)}), bf16[128,1024]{1,0:T(8,128)(2,1)}) %reduce-scatter.3.cloned.1.call-update) | async-done | bytes 262160 | tf_op jit(solution)/shard_map/reduce_scatter | solution.py:215
  442.1 41.3 %all-gather.8.cloned.1.call-done = bf16[1024,1024]{1,0:T(8,128)(2,1)} async-done(((bf16[128,1024]{1,0:T(8,128)(2,1)}), bf16[1024,1024]{1,0:T(8,128)(2,1)}) %all-gather.8.cloned.1.call-update) | async-done | bytes 2097168 | tf_op jit(solution)/shard_map/all_gather | solution.py:229
  483.4 9.0 %convolution_convert_fusion.1 = bf16[1024,1024]{1,0:T(8,128)(2,1)} fusion(bf16[512,1024]{1,0:T(8,128)(2,1)S(1)} %copy-done, bf16[1024,1024]{1,0:T(8,128)(2,1)} %all-gather.8.cloned.1.call-done, bf16[1024,512]{1,0:T(8,128)(2,1)S(1)} %copy-done.27, f32[512]{0:T(512)S(1)} %convert_element_type.89), kind=kOutput, calls=%fused_computation.81 | convolution fusion | flops 2183135232 | bytes 6293504 | tf_op jit(solution)/shard_map/dot_general | solution.py:235
  494.3 41.7 %reduce-scatter.5.cloned.1.call-done = bf16[128,1024]{1,0:T(8,128)(2,1)} async-done(((bf16[1024,1024]{1,0:T(8,128)(2,1)}), bf16[128,1024]{1,0:T(8,128)(2,1)}) %reduce-scatter.5.cloned.1.call-update) | async-done | bytes 262160 | tf_op jit(solution)/shard_map/reduce_scatter | solution.py:234
  (286 shorter events, 131.3 us)
Async XLA Ops:
  8.0 475.4 %copy-start = (bf16[512,1024]{1,0:T(8,128)(2,1)S(1)}, bf16[512,1024]{1,0:T(8,128)(2,1)}, u32[]{:S(2)}) copy-start(bf16[512,1024]{1,0:T(8,128)(2,1)} %param.33) | copy-start | bytes 3145732
  8.0 2.8 copy-start.1
  8.0 3.5 copy-start.2
  8.0 49.7 %all-gather.6.cloned.1.call-start = ((), (), s32[]{:S(2)}) async-start(), calls=%async_computation.6 | async-start | bytes 2359296 | tf_op jit(solution)/shard_map/all_gather | solution.py:66
  62.2 16.7 %copy-start.12 = (bf16[2,2,384,128]{3,2,1,0:T(8,128)(2,1)S(1)}, bf16[2,2,384,128]{3,2,1,0:T(8,128)(2,1)}, u32[]{:S(2)}) copy-start(bf16[2,2,384,128]{3,2,1,0:T(8,128)(2,1)} %param.38) | copy-start | bytes 1179652
  63.4 16.6 %copy-start.28 = (s32[128]{0:T(128)S(1)}, s32[128]{0:T(128)}, u32[]{:S(2)}) copy-start(s32[128]{0:T(128)} %param.40) | copy-start | bytes 1540
  63.4 16.7 %copy-start.17 = (s32[4]{0:T(128)S(1)}, s32[4]{0:T(128)}, u32[]{:S(2)}) copy-start(s32[4]{0:T(128)} %param.39) | copy-start | bytes 52
  63.4 43.6 %all-to-all-start = ((bf16[64,2,32,128]{3,2,1,0:T(8,128)(2,1)}), bf16[64,2,32,128]{3,2,1,0:T(8,128)(2,1)}, u32[]{:S(2)}, u32[]{:S(2)}) async-start(bf16[64,2,32,128]{3,2,1,0:T(8,128)(2,1)} %bitcast.57), calls=%async_computation | async-start | bytes 2097152 | tf_op jit(solution)/shard_map/all_to_all | solution.py:144
  77.6 192.1 %all-gather.4.cloned.1.call-start = ((), (), s32[]{:S(2)}) async-start(), calls=%async_computation.5 | async-start | bytes 2129920 | tf_op jit(solution)/shard_map/all_gather | solution.py:81
  83.7 5.1 copy-start.5
  88.7 23.2 %copy-start.14 = (bf16[1,2,384,128]{2,3,1,0:T(8,128)(2,1)S(1)}, bf16[1,2,384,128]{2,3,1,0:T(8,128)(2,1)}, u32[]{:S(2)}) copy-start(bf16[1,2,384,128]{2,3,1,0:T(8,128)(2,1)} %copy.135) | copy-start | bytes 589828
  153.1 21.3 %all-to-all-start.1 = ((f32[64,1,128]{2,1,0:T(1,128)}), f32[64,1,128]{2,1,0:T(1,128)S(1)}, u32[]{:S(2)}, u32[]{:S(2)}) async-start(f32[64,1,128]{2,1,0:T(1,128)} %reshape.304), calls=%async_computation.1 | async-start | bytes 65536 | tf_op jit(solution)/shard_map/all_to_all | solution.py:179
  175.0 207.3 %all-to-all-start.2 = ((f32[64,2,32,128]{3,2,1,0:T(8,128)}), f32[64,2,32,128]{3,2,1,0:T(8,128)}, u32[]{:S(2)}, u32[]{:S(2)}) async-start(f32[64,2,32,128]{3,2,1,0:T(8,128)} %bitcast.197), calls=%async_computation.2 | async-start | bytes 4194304 | tf_op jit(solution)/shard_map/all_to_all | solution.py:178
  181.4 256.5 %reduce-scatter.3.cloned.1.call-start = ((), (), s32[]{:S(2)}) async-start(), calls=%async_computation.7 | async-start | bytes 2359296 | tf_op jit(solution)/shard_map/reduce_scatter | solution.py:215
  273.6 2.8 copy-start.3
  292.2 4.0 copy-start.25
  300.2 2.8 copy-start.3
  318.8 4.1 copy-start.25
  326.8 2.8 copy-start.3
  345.4 4.1 copy-start.25
  353.4 2.8 copy-start.3
  372.0 4.1 copy-start.25
  387.4 5.3 copy-start.7
  387.4 5.3 copy-start.9
  387.4 5.3 copy-start.16
  392.6 4.9 copy-start.13
  397.5 40.3 %copy-start.6 = (bf16[4,32,1024]{2,1,0:T(8,128)(2,1)S(1)}, bf16[4,32,1024]{2,1,0:T(8,128)(2,1)}, u32[]{:S(2)}) copy-start(bf16[4,32,1024]{2,1,0:T(8,128)(2,1)} %param.25) | copy-start | bytes 786436
  399.6 42.5 %copy-start.26 = (bf16[512]{0:T(512)(128)(2,1)S(1)}, bf16[512]{0:T(512)(128)(2,1)}, u32[]{:S(2)}) copy-start(bf16[512]{0:T(512)(128)(2,1)} %param.32) | copy-start | bytes 3076
  399.6 83.8 %copy-start.27 = (bf16[1024,512]{1,0:T(8,128)(2,1)S(1)}, bf16[1024,512]{1,0:T(8,128)(2,1)}, u32[]{:S(2)}) copy-start(bf16[1024,512]{1,0:T(8,128)(2,1)} %param.31) | copy-start | bytes 3145732
  399.6 83.8 %all-gather.8.cloned.1.call-start = ((), (), s32[]{:S(2)}) async-start(), calls=%async_computation.8 | async-start | bytes 2359296 | tf_op jit(solution)/shard_map/all_gather | solution.py:229
  442.0 94.0 %reduce-scatter.5.cloned.1.call-start = ((), (), s32[]{:S(2)}) async-start(), calls=%async_computation.9 | async-start | bytes 2359296 | tf_op jit(solution)/shard_map/reduce_scatter | solution.py:234
  492.4 43.6 %copy-start.4 = (bf16[128,1024]{1,0:T(8,128)(2,1)S(1)}, bf16[128,1024]{1,0:T(8,128)(2,1)}, u32[]{:S(2)}) copy-start(bf16[128,1024]{1,0:T(8,128)(2,1)} %add_convert_fusion.1) | copy-start | bytes 786436
  (14 other events, 19.8 us)
Sparse Core Ops, SparseCore 0:
  10.9 46.7 all-gather.5
  399.7 38.0 reduce-scatter.2
  442.1 41.2 all-gather.7
  492.6 43.3 reduce-scatter.4
Sparse Core Ops, SparseCore 1:
  82.4 187.2 all-gather.3
where the time goes:
time: 549 us; the launch traced here: 547 us
  waiting for transfers between devices  284 us (52%)
  local copies, waits for them, and re-layouts  110 us (20%)
  matrix products  61.6 us (11%)
  other arithmetic  46.7 us (9%)
  starting transfers between devices  28.8 us (5%)
  between operations  15.7 us (3%)
    all_gather x1, waiting for transfers between devices, on_device(): roots_all = lax.all_gather(root_cache, 'owner', axis=2, tiled=True)  88.1 us
    all_gather x1, waiting for transfers between devices, on_device(): shard_rows = lax.all_gather(tokens, 'blk', axis=0, tiled=True)  44.8 us
    reduce_scatter x1, waiting for transfers between devices, on_device(): lax.psum_scatter(jnp.dot(hidden, w_down, preferred_element_type=jnp.float...  41.7 us
    all_gather x1, waiting for transfers between devices, on_device(): lax.all_gather(first_norm, 'blk', axis=0, tiled=True)  41.3 us
    reduce_scatter x1, waiting for transfers between devices, on_device(): lax.psum_scatter(jnp.dot(attn_flat, w_out, preferred_element_type=jnp.flo...  38.1 us
    all_to_all x1, waiting for transfers between devices, on_device(): lax.all_to_all(outgoing, 'owner', split_axis=0, concat_axis=0, tiled=True)  18.2 us
    select_n x4, local copies, waits for them, and re-layouts, root_block(): jnp.take(value_rows, tenant, axis=0)  16.4 us
    select_n x4, local copies, waits for them, and re-layouts, root_block(): jnp.take(key_rows, tenant, axis=0)  16.4 us
  transfers between devices with their start and end apart: 8, of which 7 were waited for; matrix products, arithmetic and copies ran while one was open for 32% of the time, Pallas kernels for 0%

commit v1 on v0

--- a/solution.py
+++ b/solution.py
@@ -7,6 +7,11 @@
 HD = 64
 norm_eps = 1e-05
 masked_score = -1e30
+
+
+def gather_over(shard, mesh_axis, d):
+    sent = jnp.stack([shard] * lax.axis_size(mesh_axis))
+    return jnp.concatenate(lax.all_to_all(sent, mesh_axis, 0, 0), axis=d)
 
 
 def layer_norm(values, gain, shift):
@@ -226,9 +231,7 @@
         shift1,
     ).astype(jnp.bfloat16)
     inner_act = jnp.dot(
-        lax.all_gather(first_norm, "blk", axis=0, tiled=True),
-        w_up,
-        preferred_element_type=jnp.float32,
+        gather_over(first_norm, "blk", 0), w_up, preferred_element_type=jnp.float32
     ) + b_up.astype(jnp.float32)
     hidden = jax.nn.gelu(inner_act, approximate=False).astype(jnp.bfloat16)
     down_sum = lax.psum_scatter(

time: 549 us -> 561 us (1.022)
  waiting for transfers between devices: 284 us -> 291 us
    all_to_all x0 -> x1, waiting for transfers between devices: none -> 48.9 us  [gather_over(): return jnp.concatenate(lax.all_to_all(sent, mesh_axis, 0, 0), axis=d)]
    all_gather x1 -> x0, waiting for transfers between devices: 41.3 us -> none  [on_device(): lax.all_gather(first_norm, 'blk', axis=0, tiled=True)]
where the time goes in v1:
time: 561 us; the launch traced here: 559 us
  waiting for transfers between devices  291 us (52%)
  local copies, waits for them, and re-layouts  111 us (20%)
  matrix products  61.6 us (11%)
  other arithmetic  46.2 us (8%)
  starting transfers between devices  32.5 us (6%)
  between operations  15.7 us (3%)
    all_gather x1, waiting for transfers between devices, on_device(): roots_all = lax.all_gather(root_cache, 'owner', axis=2, tiled=True)  88.1 us
    all_to_all x1, waiting for transfers between devices, gather_over(): return jnp.concatenate(lax.all_to_all(sent, mesh_axis, 0, 0), axis=d)  48.9 us
    all_gather x1, waiting for transfers between devices, on_device(): shard_rows = lax.all_gather(tokens, 'blk', axis=0, tiled=True)  44.8 us
    reduce_scatter x1, waiting for transfers between devices, on_device(): lax.psum_scatter(jnp.dot(hidden, w_down, preferred_element_type=jnp.float...  41.5 us
    reduce_scatter x1, waiting for transfers between devices, on_device(): lax.psum_scatter(jnp.dot(attn_flat, w_out, preferred_element_type=jnp.flo...  38 us
    all_to_all x1, waiting for transfers between devices, on_device(): lax.all_to_all(outgoing, 'owner', split_axis=0, concat_axis=0, tiled=True)  18.4 us
    select_n x4, local copies, waits for them, and re-layouts, root_block(): jnp.take(value_rows, tenant, axis=0)  16.3 us
    select_n x4, other arithmetic, root_block(): jnp.take(value_rows, tenant, axis=0)  16.3 us
  transfers between devices with their start and end apart: 8, of which 7 were waited for; matrix products, arithmetic and copies ran while one was open for 32% of the time, Pallas kernels for 0%

profile of v1, /device:TPU:2, one launch (start us, length us, event | category | flops | bytes accessed | tf_op | source)
XLA Modules:
  0.0 559.1 jit_solution(5901508390413226402)
XLA Ops:
  13.0 44.8 %all-gather.5.cloned.1.call-done = bf16[32,32,1024]{2,1,0:T(8,128)(2,1)} async-done(((bf16[4,32,1024]{2,1,0:T(8,128)(2,1)}), bf16[32,32,1024]{2,1,0:T(8,128)(2,1)}) %all-gather.5.cloned.1.call-update) | async-done | bytes 2097168 | tf_op jit(solution)/shard_map/all_gather | solution.py:71
  63.4 14.2 %all-to-all-start = ((bf16[64,2,32,128]{3,2,1,0:T(8,128)(2,1)}), bf16[64,2,32,128]{3,2,1,0:T(8,128)(2,1)}, u32[]{:S(2)}, u32[]{:S(2)}) async-start(bf16[64,2,32,128]{3,2,1,0:T(8,128)(2,1)} %bitcast.58), calls=%async_computation | async-start | bytes 2097152 | tf_op jit(solution)/shard_map/all_to_all | solution.py:149
  88.6 18.4 %all-to-all-done = bf16[64,2,32,128]{3,2,1,0:T(8,128)(2,1)} async-done(((bf16[64,2,32,128]{3,2,1,0:T(8,128)(2,1)}), bf16[64,2,32,128]{3,2,1,0:T(8,128)(2,1)}, u32[]{:S(2)}, u32[]{:S(2)}) %all-to-all-start) | async-done | bytes 1048608 | tf_op jit(solution)/shard_map/all_to_all | solution.py:149
  107.0 5.0 reshape.210
  111.9 39.3 %while.31 = (s32[]{:T(128)}, f32[8,8,2,32,128]{4,3,2,1,0:T(8,128)}, f32[8,8,2,32,2]{3,1,0,4,2:T(8,128)}, bf16[8,8,2,32,2,64]{5,4,3,2,1,0:T(2,128)(2,1)}, bf16[2,...) while((s32[]{:T(128)}, f32[8,8,2,32,128]{4,3,2,1,0:T(8,128)}, ...), condition=%wide.region_8.10_spmd.clone, body=%wide.region_5.9_spmd.clone.sunk | while | flops 104267520 | bytes 7389281 | solution.py:180
  153.0 7.9 %all-to-all-start.1 = ((f32[64,1,128]{2,1,0:T(1,128)}), f32[64,1,128]{2,1,0:T(1,128)S(1)}, u32[]{:S(2)}, u32[]{:S(2)}) async-start(f32[64,1,128]{2,1,0:T(1,128)} %reshape.310), calls=%async_computation.1 | async-start | bytes 65536 | tf_op jit(solution)/shard_map/all_to_all | solution.py:184
  163.8 10.5 %all-to-all-done.1 = f32[64,1,128]{2,1,0:T(1,128)S(1)} async-done(((f32[64,1,128]{2,1,0:T(1,128)}), f32[64,1,128]{2,1,0:T(1,128)S(1)}, u32[]{:S(2)}, u32[]{:S(2)}) %all-to-all-start.1) | async-done | bytes 32800 | tf_op jit(solution)/shard_map/all_to_all | solution.py:184
  174.9 6.4 %all-to-all-start.2 = ((f32[64,2,32,128]{3,2,1,0:T(8,128)}), f32[64,2,32,128]{3,2,1,0:T(8,128)}, u32[]{:S(2)}, u32[]{:S(2)}) async-start(f32[64,2,32,128]{3,2,1,0:T(8,128)} %bitcast.198), calls=%async_computation.2 | async-start | bytes 4194304 | tf_op jit(solution)/shard_map/all_to_all | solution.py:183
  181.5 88.1 %all-gather.3.cloned.1.call-done = bf16[2,4,1024,128]{3,2,1,0:T(8,128)(2,1)} async-done(((bf16[2,4,16,128]{3,2,1,0:T(8,128)(2,1)}), bf16[2,4,1024,128]{3,2,1,0:T(8,128)(2,1)}) %all-gather.3.cloned.1.call-update) | async-done | bytes 2097168 | tf_op jit(solution)/shard_map/all_gather | solution.py:86
  269.6 106.3 %while.32 = (s32[]{:T(128)}, f32[32,32,2]{1,2,0:T(2,128)S(1)}, f32[32,32,2]{1,2,0:T(2,128)S(1)}, f32[32,32,2,64]{3,1,2,0:T(8,128)}, s32[32]{0:T(128)S(1)}, /*ind...) while((s32[]{:T(128)}, f32[32,32,2]{1,2,0:T(2,128)S(1)}, ...), condition=%wide.region_3.5_spmd.clone, body=%wide.region_0.4_spmd.clone.sunk | while | flops 143543840 | bytes 50766020 | solution.py:125
  276.5 4.1 broadcast_select_fusion.4
  280.6 4.1 copy.240
  288.1 4.1 copy.241
  292.2 3.9 fusion.189
  303.0 4.1 broadcast_select_fusion.4
  307.1 4.1 copy.240
  314.6 4.1 copy.241
  318.7 4.0 fusion.189
  329.6 4.1 broadcast_select_fusion.4
  333.7 4.1 copy.240
  341.2 4.1 copy.241
  345.3 4.0 fusion.189
  356.2 4.1 broadcast_select_fusion.4
  360.3 4.1 copy.240
  367.8 4.1 copy.241
  371.9 4.0 fusion.189
  387.4 5.2 fusion.43
  392.7 4.0 fusion.46
  399.7 38.0 %reduce-scatter.3.cloned.1.call-done = bf16[128,1024]{1,0:T(8,128)(2,1)} async-done(((bf16[1024,1024]{1,0:T(8,128)(2,1)}), bf16[128,1024]{1,0:T(8,128)(2,1)}) %reduce-scatter.3.cloned.1.call-update) | async-done | bytes 262160 | tf_op jit(solution)/shard_map/reduce_scatter | solution.py:220
  446.5 48.9 %all-to-all-done.3 = bf16[8,128,1024]{2,1,0:T(8,128)(2,1)S(1)} async-done(((bf16[8,128,1024]{2,1,0:T(8,128)(2,1)}), bf16[8,128,1024]{2,1,0:T(8,128)(2,1)S(1)}, u32[]{:S(2)}, u32[]{:S(2)}) %all-to-all-start.3) | async-done | bytes 2097184 | tf_op jit(solution)/shard_map/all_to_all | solution.py:14
  495.4 9.0 %convolution_convert_fusion.1 = bf16[1024,1024]{1,0:T(8,128)(2,1)} fusion(bf16[512,1024]{1,0:T(8,128)(2,1)S(1)} %copy-done, bf16[1024,1024]{1,0:T(8,128)(2,1)S(1)} %bitcast.201, bf16[1024,512]{1,0:T(8,128)(2,1)} %param.31, f32[512]{0:T(512)S(1)} %convert_element_type.89), kind=kOutput, calls=%fused_computation.81 | convolution fusion | flops 2183135232 | bytes 6293504 | tf_op jit(solution)/shard_map/dot_general | solution.py:238
  506.4 41.5 %reduce-scatter.5.cloned.1.call-done = bf16[128,1024]{1,0:T(8,128)(2,1)} async-done(((bf16[1024,1024]{1,0:T(8,128)(2,1)}), bf16[128,1024]{1,0:T(8,128)(2,1)}) %reduce-scatter.5.cloned.1.call-update) | async-done | bytes 262160 | tf_op jit(solution)/shard_map/reduce_scatter | solution.py:237
  (282 shorter events, 136.0 us)
Async XLA Ops:
  8.0 487.4 %copy-start = (bf16[512,1024]{1,0:T(8,128)(2,1)S(1)}, bf16[512,1024]{1,0:T(8,128)(2,1)}, u32[]{:S(2)}) copy-start(bf16[512,1024]{1,0:T(8,128)(2,1)} %param.33) | copy-start | bytes 3145732
  8.0 2.8 copy-start.1
  8.0 3.5 copy-start.2
  8.0 49.7 %all-gather.5.cloned.1.call-start = ((), (), s32[]{:S(2)}) async-start(), calls=%async_computation.7 | async-start | bytes 2359296 | tf_op jit(solution)/shard_map/all_gather | solution.py:71
  62.2 16.7 %copy-start.11 = (bf16[2,2,384,128]{3,2,1,0:T(8,128)(2,1)S(1)}, bf16[2,2,384,128]{3,2,1,0:T(8,128)(2,1)}, u32[]{:S(2)}) copy-start(bf16[2,2,384,128]{3,2,1,0:T(8,128)(2,1)} %param.38) | copy-start | bytes 1179652
  63.4 16.6 %copy-start.26 = (s32[128]{0:T(128)S(1)}, s32[128]{0:T(128)}, u32[]{:S(2)}) copy-start(s32[128]{0:T(128)} %param.40) | copy-start | bytes 1540
  63.4 16.8 %copy-start.16 = (s32[4]{0:T(128)S(1)}, s32[4]{0:T(128)}, u32[]{:S(2)}) copy-start(s32[4]{0:T(128)} %param.39) | copy-start | bytes 52
  63.4 43.6 %all-to-all-start = ((bf16[64,2,32,128]{3,2,1,0:T(8,128)(2,1)}), bf16[64,2,32,128]{3,2,1,0:T(8,128)(2,1)}, u32[]{:S(2)}, u32[]{:S(2)}) async-start(bf16[64,2,32,128]{3,2,1,0:T(8,128)(2,1)} %bitcast.58), calls=%async_computation | async-start | bytes 2097152 | tf_op jit(solution)/shard_map/all_to_all | solution.py:149
  77.6 192.1 %all-gather.3.cloned.1.call-start = ((), (), s32[]{:S(2)}) async-start(), calls=%async_computation.6 | async-start | bytes 2129920 | tf_op jit(solution)/shard_map/all_gather | solution.py:86
  83.5 5.1 copy-start.4
  88.6 23.4 %copy-start.13 = (bf16[1,2,384,128]{2,3,1,0:T(8,128)(2,1)S(1)}, bf16[1,2,384,128]{2,3,1,0:T(8,128)(2,1)}, u32[]{:S(2)}) copy-start(bf16[1,2,384,128]{2,3,1,0:T(8,128)(2,1)} %copy.135) | copy-start | bytes 589828
  153.0 21.3 %all-to-all-start.1 = ((f32[64,1,128]{2,1,0:T(1,128)}), f32[64,1,128]{2,1,0:T(1,128)S(1)}, u32[]{:S(2)}, u32[]{:S(2)}) async-start(f32[64,1,128]{2,1,0:T(1,128)} %reshape.310), calls=%async_computation.1 | async-start | bytes 65536 | tf_op jit(solution)/shard_map/all_to_all | solution.py:184
  174.9 207.4 %all-to-all-start.2 = ((f32[64,2,32,128]{3,2,1,0:T(8,128)}), f32[64,2,32,128]{3,2,1,0:T(8,128)}, u32[]{:S(2)}, u32[]{:S(2)}) async-start(f32[64,2,32,128]{3,2,1,0:T(8,128)} %bitcast.198), calls=%async_computation.2 | async-start | bytes 4194304 | tf_op jit(solution)/shard_map/all_to_all | solution.py:183
  181.3 256.4 %reduce-scatter.3.cloned.1.call-start = ((), (), s32[]{:S(2)}) async-start(), calls=%async_computation.8 | async-start | bytes 2359296 | tf_op jit(solution)/shard_map/reduce_scatter | solution.py:220
  273.6 2.9 copy-start.3
  292.2 4.0 copy-start.24
  300.1 2.9 copy-start.3
  318.7 4.0 copy-start.24
  326.7 2.9 copy-start.3
  345.3 4.0 copy-start.24
  353.3 2.9 copy-start.3
  371.9 4.0 copy-start.24
  387.4 5.3 copy-start.6
  387.4 5.3 copy-start.8
  387.4 5.3 copy-start.15
  392.7 4.9 copy-start.12
  397.6 2.1 copy-start.18
  397.6 2.1 copy-start.19
  397.6 40.1 %copy-start.5 = (bf16[4,32,1024]{2,1,0:T(8,128)(2,1)S(1)}, bf16[4,32,1024]{2,1,0:T(8,128)(2,1)}, u32[]{:S(2)}) copy-start(bf16[4,32,1024]{2,1,0:T(8,128)(2,1)} %param.25) | copy-start | bytes 786436
  442.7 3.8 copy-start.25
  442.7 52.7 %all-to-all-start.3 = ((bf16[8,128,1024]{2,1,0:T(8,128)(2,1)}), bf16[8,128,1024]{2,1,0:T(8,128)(2,1)S(1)}, u32[]{:S(2)}, u32[]{:S(2)}) async-start(bf16[8,128,1024]{2,1,0:T(8,128)(2,1)} %stack.8), calls=%async_computation.4 | async-start | bytes 4194304 | tf_op jit(solution)/shard_map/all_to_all | solution.py:14
  446.4 101.4 %reduce-scatter.5.cloned.1.call-start = ((), (), s32[]{:S(2)}) async-start(), calls=%async_computation.9 | async-start | bytes 2359296 | tf_op jit(solution)/shard_map/reduce_scatter | solution.py:237
  (12 other events, 15.4 us)
Sparse Core Ops, SparseCore 0:
  10.9 46.7 all-gather.4
  399.8 37.8 reduce-scatter.2
  504.6 43.2 reduce-scatter.4
Sparse Core Ops, SparseCore 1:
  82.4 187.2 all-gather.2
